TPU v7x, 32 devices: a whole 2x2x4 slice. The times are simulated.
32 devices in a mesh: groups: 2 (over x), tile: 16 (over z, y, core).
Axes of the slice: x: 2, y: 2, z: 4, core: 2. Of those that a mesh axis runs over, the one named last changes fastest.
Arguments:
- tiles: float32 [2, 12288, 384], P(None, ('groups', 'tile')), parts along dimension 1, may hold values from -6 to 6
- library: float32 [128, 2, 128, 128], P('tile'), may hold values from -6 to 6
- block_owner: int32 [2], replicated, may hold values from 0 to 15
- block_clips: int32 [2, 2], replicated, may hold values from 0 to 7
- layer_order: int32 [32, 2], P(('groups', 'tile')), parts along dimension 0, may hold values from 0 to 1, each once within a row
Outputs:
- scores: float32 [2, 2, 12288, 384], P(None, None, ('groups', 'tile')), parts along dimension 2
- peak_scores: float32 [4, 2], P('groups'), parts along dimension 0
There are 2 independent parts, one for each index of `groups`. A program takes and returns all parts, laid end to end along the dimension named above; an argument that names none is the same for every part. Nothing has to cross between parts.
Inputs may be any that keep to these rules, and one draw needn't show every extreme that they name: `layer_order`: each row is a permutation of 0 to 1.
All inputs are finite; a program needn't handle non-finite values.
Results may differ from a plain program's by a relative error of at most 0.000098.
Values sent between devices are 32-bit elements; how exact they have to be, the bound alone decides.
A program may use at most 128 MiB of HBM per device.

v0:
```python
import functools
import math

import jax
import jax.numpy as jnp
import numpy as np
from jax import lax
from jax.experimental import pallas as pl
from jax.experimental.pallas import tpu as pltpu
from jax.sharding import PartitionSpec as P

F32 = jnp.float32
BF16 = jnp.bfloat16


def from_behind(block, axis):
    devices = range(lax.axis_size(axis))
    return lax.ppermute(block, axis, [(i + 1, i) for i in devices if i + 1 in devices])


def split(x):
    high = x.astype(BF16)
    return high, (x - high.astype(F32)).astype(BF16)


def mm(a, b):
    return jnp.dot(a, b, preferred_element_type=F32)


def transform_matrix(extent):
    span = 2 * extent
    odd = 2 * np.arange(extent)[:, None] + 1
    angle = (odd * np.arange(span)[None, :] % (2 * span)) * (math.pi / span)
    return np.concatenate([np.cos(angle), np.sin(angle)], axis=0).astype(np.float32)


def halves(matrix):
    high = matrix.astype(BF16)
    low = (matrix - high.astype(np.float32)).astype(BF16)
    return high, low


def constants(extent):
    forward = transform_matrix(extent)
    fh, fl = halves(forward)
    row_left = np.concatenate([fh, fl, fh], axis=1)
    ft = np.ascontiguousarray(forward.T)
    th, tl = halves(ft)
    col_right = np.stack([th, tl])
    back = forward[:, :extent] * np.float32(1.0 / extent)
    bh, bl = halves(back)
    back_right = np.stack([bh, bl])
    back_left = np.concatenate([bh.T, bl.T, bh.T], axis=1)
    offset = np.arange(2 * extent)[None, :] - np.arange(extent)[:, None]
    band = ((offset >= 0) & (offset < extent)).astype(BF16)
    band_left = np.concatenate([band, band], axis=1)
    band_right = np.ascontiguousarray(band.T)
    return [jnp.asarray(c) for c in (row_left, col_right, back_left, back_right, band_left, band_right)]


def combine(y, e):
    a, b = y[:e, :e], y[:e, e:]
    c, d = y[e:, :e], y[e:, e:]
    return a - d, b + c, a + d, c - b


def kernel(order, tiles, halo, clips, row_left, col_right, back_left, back_right, band_left, band_right,
           scores, peaks, yh, yl, inv, spectra, wh, wl):
    layers, rows, cols = tiles.shape
    blocks, per_block = clips.shape[:2]
    count = blocks * per_block
    e = clips.shape[-1]
    span = 2 * e
    nr, nc = rows // e, cols // e
    entries = layers * e * e

    clip_scale = []
    for k in range(count):
        total = jnp.zeros((e, e), F32)
        for l in range(layers):
            chosen = clips[k // per_block, k % per_block, order[0, l]]
            total = total + chosen * chosen
            ch, cl = split(chosen)
            first = mm(row_left[:, :e], ch) + mm(row_left[:, span:span + e], ch) + mm(row_left[:, :e], cl)
            fh, fl = split(first)
            second = mm(fh, col_right[0, :e]) + mm(fl, col_right[0, :e]) + mm(fh, col_right[1, :e])
            for n, part in enumerate(combine(second, e)):
                spectra[k, l, n] = part
        mean = jnp.sum(total, keepdims=True) / entries
        clip_scale.append(1.0 / (math.sqrt(entries) * jnp.sqrt(mean + 1e-05)))

    for b in range(nr):
        squares = None
        for l in range(layers):
            if b + 2 <= nr:
                x = tiles[l, b * e:(b + 2) * e]
            else:
                x = jnp.concatenate([tiles[l, b * e:], halo[l]], axis=0)
            squares = x * x if squares is None else squares + x * x
            xh, xl = split(x)
            y = mm(row_left[...], jnp.concatenate([xh, xh, xl], axis=0))
            h, low = split(y)
            yh[b, l], yl[b, l] = h, low
        sh, sl = split(squares)
        energy = mm(band_left[...], jnp.concatenate([sh, sl], axis=0))
        eh, el = split(energy)
        for c in range(nc):
            width = min(2, nc - c) * e
            at = slice(c * e, c * e + width)
            window = mm(eh[:, at], band_right[:width]) + mm(el[:, at], band_right[:width])
            inv[b, :, c * e:(c + 1) * e] = 1.0 / jnp.sqrt(window / entries + 1e-05)

    for k in range(count):
        peaks[k:k + 1] = jnp.full((1, e), -jnp.inf, F32)

    def row_block(b, carry):
        for c in range(nc):
            width = min(2, nc - c) * e
            at = slice(c * e, c * e + width)
            tile_parts = []
            for l in range(layers):
                h, low = yh[b, l, :, at], yl[b, l, :, at]
                y = mm(h, col_right[0, :width]) + mm(low, col_right[0, :width]) + mm(h, col_right[1, :width])
                tile_parts.append(combine(y, e))
            for k in range(count):
                u1 = u2 = v1 = v2 = None
                for l in range(layers):
                    p1, p2, q1, q2 = tile_parts[l]
                    c1, c2, d1, d2 = (spectra[k, l, n] for n in range(4))
                    t = (p1 * c1 + p2 * c2, p2 * c1 - p1 * c2, q1 * d1 + q2 * d2, q2 * d1 - q1 * d2)
                    if u1 is None:
                        u1, u2, v1, v2 = t
                    else:
                        u1, u2, v1, v2 = u1 + t[0], u2 + t[1], v1 + t[2], v2 + t[3]
                z = jnp.concatenate([
                    jnp.concatenate([u1 + v1, u2 - v2], axis=1),
                    jnp.concatenate([u2 + v2, v1 - u1], axis=1)], axis=0)
                zh, zl = split(z)
                w = mm(zh, back_right[0]) + mm(zl, back_right[0]) + mm(zh, back_right[1])
                h, low = split(w)
                wh[k, :, c * e:(c + 1) * e] = h
                wl[k, :, c * e:(c + 1) * e] = low
        scale = inv[b]
        for k in range(count):
            out = mm(back_left[...], jnp.concatenate([wh[k], wh[k], wl[k]], axis=0))
            out = out * scale * (clip_scale[k] * 0.5)
            scores[k // per_block, k % per_block, pl.ds(pl.multiple_of(b * e, e), e)] = out
            top = jnp.max(out, axis=0, keepdims=True)
            best = peaks[k:k + 1]
            for c in range(nc):
                best = jnp.maximum(best, top[:, c * e:(c + 1) * e])
            peaks[k:k + 1] = best
        return carry

    lax.fori_loop(0, nr, row_block, 0)


def correlate(tiles, halo, clips, order):
    layers, rows, cols = tiles.shape
    blocks, per_block = clips.shape[:2]
    e = clips.shape[-1]
    span = 2 * e
    nr = rows // e
    count = blocks * per_block
    vmem = pl.BlockSpec(memory_space=pltpu.VMEM)
    return pl.pallas_call(
        kernel,
        out_shape=(jax.ShapeDtypeStruct((blocks, per_block, rows, cols), F32),
                   jax.ShapeDtypeStruct((count, e), F32)),
        in_specs=[pl.BlockSpec(memory_space=pltpu.SMEM)] + [vmem] * 9,
        out_specs=(vmem, vmem),
        scratch_shapes=[
            pltpu.VMEM((nr, layers, span, cols), BF16),
            pltpu.VMEM((nr, layers, span, cols), BF16),
            pltpu.VMEM((nr, e, cols), F32),
            pltpu.VMEM((count, layers, 4, e, e), F32),
            pltpu.VMEM((count, span, cols), BF16),
            pltpu.VMEM((count, span, cols), BF16),
        ],
        compiler_params=pltpu.CompilerParams(vmem_limit_bytes=60 * 1024 * 1024),
    )(order, tiles, halo, clips, *constants(e))


def local(tiles, library, block_owner, block_clips, layer_order):
    e = library.shape[-1]
    halo = from_behind(tiles[:, :e, :], "tile")
    picked = library[block_clips]
    owned = block_owner == lax.axis_index("tile")
    delivered = lax.psum(jnp.where(owned[:, None, None, None, None], picked, 0.0), "tile")
    scores, peaks = correlate(tiles, halo, delivered, layer_order)
    peak = lax.pmax(jnp.max(peaks, axis=1), "tile").reshape(block_clips.shape)
    return scores, peak


def solution(mesh):
    in_specs = (
        P(None, ("groups", "tile"), None),
        P("tile", None, None, None),
        P(),
        P(),
        P(("groups", "tile"), None),
    )
    out_specs = (P(None, None, ("groups", "tile"), None), P("groups", None))
    return jax.shard_map(local, mesh=mesh, in_specs=in_specs, out_specs=out_specs, check_vma=False)
```

profile of v0, /device:TPU:0, one launch (start us, length us, event | category | flops | bytes accessed | tf_op | source)
XLA Modules:
  0.0 164.8 jit_solution(6948527090679653291)
XLA Ops:
  7.2 0.0 copy-start
  7.2 0.0 all-reduce.2.cloned.1.call-start
  7.2 1.1 slice.3
  8.3 1.3 collective-permute-start
  9.6 0.7 compare_select_fusion
  10.3 0.1 reshape.11
  10.4 0.7 broadcast_compare_fusion
  11.1 0.0 copy-done
  11.1 0.6 gather_fusion
  11.7 0.9 broadcast_select_fusion
  12.6 0.0 all-reduce.2.cloned.1.call-update
  12.6 94.4 %all-reduce.2.cloned.1.call-done.clips = f32[2,2,2,128,128]{4,3,2,1,0:T(8,128)} async-done(((f32[2,2,2,128,128]{4,3,2,1,0:T(8,128)}), f32[2,2,2,128,128]{4,3,2,1,0:T(8,128)}) %all-reduce.2.cloned.1.call-update) | async-done | bytes 524304 | tf_op jit(solution)/shard_map/psum | solution.py:189
  107.0 0.0 collective-permute-done.halo
  107.0 0.0 copy-start.1
  107.0 0.8 copy-done.1
  107.7 17.0 %shard_map.122 = (f32[2,2,384,384]{3,2,1,0:T(8,128)}, f32[4,128]{1,0:T(4,128)}) custom-call(s32[1,2]{1,0:T(1,128)} %order.1, f32[2,384,384]{2,1,0:T(8,128)} %tiles.1, f32[2,128,384]{2,1,0:T(8,128)} %copy-done.1, f32[2,2,2,128,128]{4,3,2,1,0:T(8,128)} %all-reduce.2.cloned.1.call-done.clips, bf16[256,768]{1,0:T(8,128)(2,1)} %constant.24.clone.row_left, ...), custom_call_target="tpu_custom_call" | custom-call | tf_op jit(solution)/shard_map/pallas_call | solution.py:166
  124.7 0.8 reduce_max.9
  125.5 0.1 reshape.8
  125.6 32.4 %pmax.7 = f32[2,2]{1,0:T(2,128)} all-reduce(f32[2,2]{1,0:T(2,128)S(1)} %reshape.8), channel_id=1, replica_groups=mesh['groups'=2,'tile'=16] {'tile'}, use_global_device_ids=true, to_apply=%region_2.3 | all-reduce | flops 4 | bytes 32 | tf_op jit(solution)/shard_map/pmax | solution.py:191
  (1 shorter events, 0.0 us)
Async XLA Ops:
  7.2 3.9 %copy-start = (f32[8,2,128,128]{3,2,1,0:T(8,128)S(1)}, f32[8,2,128,128]{3,2,1,0:T(8,128)}, u32[]{:S(2)}) copy-start(f32[8,2,128,128]{3,2,1,0:T(8,128)} %param.12) | copy-start | bytes 3145732
  7.2 99.8 %all-reduce.2.cloned.1.call-start = ((), (), s32[]{:S(2)}) async-start(), calls=%async_computation | async-start | bytes 1048576 | tf_op jit(solution)/shard_map/psum | solution.py:189
  8.3 98.7 %collective-permute-start = (f32[2,128,384]{2,1,0:T(8,128)S(1)}, f32[2,128,384]{2,1,0:T(8,128)S(1)}, u32[]{:S(2)}, u32[]{:S(2)}) collective-permute-start(f32[2,128,384]{2,1,0:T(8,128)S(1)} %slice.3), channel_id=1, source_target_pairs={{1,0},{2,1},{3,2},{4,3},{5,4},{6,5},{7,6},{8,7},{9,8},{10,9},{11,1... | collective-permute-start | bytes 1179656 | tf_op jit(solution)/shard_map/ppermute | solution.py:18
  107.0 0.8 copy-start.1
Sparse Core Ops, SparseCore 0:
  12.7 94.2 all-reduce.1
where the time goes:
time: 165 us
  waiting for transfers between devices  94.4 us (57%)
  blocking collectives  32.4 us (20%)
  Pallas kernels  17 us (10%)
  between operations  14.1 us (9%)
  other arithmetic  3.04 us (2%)
  local copies, waits for them, and re-layouts  2.62 us (2%)
    psum x1, waiting for transfers between devices, local(): lax.psum(jnp.where(owned[:, None, None, None, None], picked, 0.0), 'tile')  94.4 us
    pmax x1, blocking collectives, local(): peak = lax.pmax(jnp.max(peaks, axis=1), 'tile').reshape(block_clips.shape)  32.4 us
    pallas_call x1, Pallas kernels, correlate(): pl.pallas_call(kernel, out_shape=(jax.ShapeDtypeStruct((blocks, per_block...  17 us
  transfers between devices with their start and end apart: 2, of which 1 were waited for; matrix products, arithmetic and copies ran while one was open for 2% of the time, Pallas kernels for 0%

commit v1 on v0

--- a/solution.py
+++ b/solution.py
@@ -11,11 +11,6 @@
 
 F32 = jnp.float32
 BF16 = jnp.bfloat16
-
-
-def from_behind(block, axis):
-    devices = range(lax.axis_size(axis))
-    return lax.ppermute(block, axis, [(i + 1, i) for i in devices if i + 1 in devices])
 
 
 def split(x):
@@ -110,8 +105,7 @@
             window = mm(eh[:, at], band_right[:width]) + mm(el[:, at], band_right[:width])
             inv[b, :, c * e:(c + 1) * e] = 1.0 / jnp.sqrt(window / entries + 1e-05)
 
-    for k in range(count):
-        peaks[k:k + 1] = jnp.full((1, e), -jnp.inf, F32)
+    peaks[...] = jnp.full(peaks.shape, -jnp.inf, F32)
 
     def row_block(b, carry):
         for c in range(nc):
@@ -166,7 +160,7 @@
     return pl.pallas_call(
         kernel,
         out_shape=(jax.ShapeDtypeStruct((blocks, per_block, rows, cols), F32),
-                   jax.ShapeDtypeStruct((count, e), F32)),
+                   jax.ShapeDtypeStruct((-(-count // 8) * 8, e), F32)),
         in_specs=[pl.BlockSpec(memory_space=pltpu.SMEM)] + [vmem] * 9,
         out_specs=(vmem, vmem),
         scratch_shapes=[
@@ -181,15 +175,244 @@
     )(order, tiles, halo, clips, *constants(e))
 
 
+MESH = pl.DeviceIdType.MESH
+PLANE = 4
+CHUNKS = 4
+
+
+def share_kernel(groups, tiles_n, owner, picks, library, tiles, full_out, halo_out,
+                 stage, landed, mine, rbuf, lbuf, rsend, lsend, full, zeros,
+                 rs_send, rs_recv, r_send, r_recv, l_send, l_recv,
+                 ag_send, ag_recv, fw_send, fw_recv, halo_send, halo_recv, zero_sem):
+    g = lax.axis_index("groups")
+    t = lax.axis_index("tile")
+    per_block = picks.shape[1]
+    layers, e = library.shape[1], library.shape[-1]
+    z = t // PLANE
+    q = lax.rem(t, PLANE)
+    depth = tiles_n // PLANE
+    parity = lax.rem(g, 2)
+    other_g = g + 1 - 2 * parity
+    core = lax.rem(q, 2)
+    partner = t + 1 - 2 * core
+    upper = q // 2
+    across = t + 2 - 4 * upper
+    plane = [z * PLANE + lax.rem(q + d, PLANE) for d in range(1, PLANE)]
+    always = [(g, other) for other in plane] + [(other_g, t), (other_g, across)]
+    sometimes = [(z > 0, (g, t - PLANE)), (z < depth - 1, (g, t + PLANE)),
+                 (t > 0, (g, t - 1)), (t < tiles_n - 1, (g, t + 1))]
+
+    barrier = pltpu.get_barrier_semaphore()
+    for target in always:
+        pl.semaphore_signal(barrier, inc=1, device_id=target, device_id_type=MESH)
+    for there, target in sometimes:
+        @pl.when(there)
+        def _(target=target):
+            pl.semaphore_signal(barrier, inc=1, device_id=target, device_id_type=MESH)
+
+    def contribution(slab):
+        clip, layer = slab // layers, lax.rem(slab, layers)
+        block, which = clip // per_block, lax.rem(clip, per_block)
+        mask = jnp.where(owner[block] == t, 1.0, 0.0).astype(F32)
+        return library[picks[block, which], layer] * mask
+
+    for d in range(PLANE):
+        stage[d] = contribution(parity * PLANE + lax.rem(q + d, PLANE))
+
+    @pl.when(z == 0)
+    def _():
+        rbuf[...] = jnp.zeros_like(rbuf)
+
+    @pl.when(z == depth - 1)
+    def _():
+        lbuf[...] = jnp.zeros_like(lbuf)
+
+    pl.semaphore_wait(barrier, len(always) + sum(jnp.where(there, 1, 0) for there, _ in sometimes))
+
+    def remote(src, dst, send, recv, target):
+        return pltpu.make_async_remote_copy(src_ref=src, dst_ref=dst, send_sem=send, recv_sem=recv,
+                                            device_id=target, device_id_type=MESH)
+
+    scatter = []
+    for d in range(1, PLANE):
+        copy = remote(stage.at[d], landed.at[d - 1], rs_send.at[d - 1], rs_recv.at[d - 1], (g, plane[d - 1]))
+        copy.start()
+        scatter.append(copy)
+    for copy in scatter:
+        copy.wait()
+    mine[...] = stage[0] + landed[0] + landed[1] + landed[2]
+
+    halo = remote(tiles.at[:, pl.ds(0, e)], halo_out, halo_send, halo_recv, (g, t - 1))
+
+    @pl.when(t > 0)
+    def _():
+        halo.start()
+
+    @pl.when(t == tiles_n - 1)
+    def _():
+        zeros[...] = jnp.zeros_like(zeros)
+        fill = pltpu.make_async_copy(zeros, halo_out, zero_sem)
+        fill.start()
+        fill.wait()
+
+    step = e // CHUNKS
+    parts = [pl.ds(c * step, step) for c in range(CHUNKS)]
+    slab = parity * PLANE + q
+    right = [remote(rsend.at[c], rbuf.at[c], r_send.at[c], r_recv.at[c], (g, t + PLANE)) for c in range(CHUNKS)]
+    left = [remote(lsend.at[c], lbuf.at[c], l_send.at[c], l_recv.at[c], (g, t - PLANE)) for c in range(CHUNKS)]
+    forwards = []
+    slabs = [slab, (1 - parity) * PLANE + q,
+             parity * PLANE + q + 2 - 4 * upper, (1 - parity) * PLANE + q + 2 - 4 * upper]
+    targets = [(other_g, t), (g, across), (other_g, across)]
+
+    def forward(n, c):
+        copy = remote(full.at[slabs[n], parts[c]], full.at[slabs[n], parts[c]],
+                      fw_send.at[n, c], fw_recv.at[n, c], (g, partner))
+        copy.start()
+        forwards.append(copy)
+
+    gathers = [(n, c, remote(full.at[slab, parts[c]], full.at[slab, parts[c]], ag_send.at[n, c], ag_recv.at[n, c], target))
+               for c in range(CHUNKS) for n, target in enumerate(targets)]
+    own = [remote(full.at[slab, parts[c]], full.at[slab, parts[c]], fw_send.at[0, c], fw_recv.at[0, c], (g, partner))
+           for c in range(CHUNKS)]
+
+    def rightward(c):
+        @pl.when(z > 0)
+        def _():
+            right[c].wait_recv()
+        rsend[c] = rbuf[c] + mine[parts[c]]
+
+        @pl.when(z < depth - 1)
+        def _():
+            right[c].start()
+
+    def leftward(c):
+        @pl.when(z < depth - 1)
+        def _():
+            left[c].wait_recv()
+        lsend[c] = lbuf[c] + mine[parts[c]]
+
+        @pl.when(z > 0)
+        def _():
+            left[c].start()
+
+    def deliver(c):
+        full[slab, parts[c]] = rsend[c] + lbuf[c]
+        for n in range(3):
+            gathers[3 * c + n][2].start()
+        own[c].start()
+
+    lower = z < depth // 2
+    for condition, first, second in ((lower, rightward, leftward), (jnp.logical_not(lower), leftward, rightward)):
+        @pl.when(condition)
+        def _(first=first, second=second):
+            for c in range(CHUNKS):
+                first(c)
+            for c in range(CHUNKS):
+                second(c)
+                deliver(c)
+    forwards.extend(own)
+    for n, c, copy in gathers:
+        copy.wait_recv()
+        forward(n + 1, c)
+    for copy in forwards:
+        copy.wait_recv()
+    full_out[...] = full[...]
+    for _, _, copy in gathers:
+        copy.wait_send()
+    for copy in forwards:
+        copy.wait_send()
+    for c in range(CHUNKS):
+        @pl.when(z < depth - 1)
+        def _(c=c):
+            right[c].wait_send()
+
+        @pl.when(z > 0)
+        def _(c=c):
+            left[c].wait_send()
+
+    @pl.when(t > 0)
+    def _():
+        halo.wait_send()
+
+    @pl.when(t < tiles_n - 1)
+    def _():
+        halo.wait_recv()
+
+
+def share(tiles, library, block_owner, block_clips):
+    layers, e = library.shape[1], library.shape[-1]
+    cols = tiles.shape[-1]
+    slabs = block_clips.size * layers
+    assert slabs == 2 * PLANE
+    groups, tiles_n = lax.axis_size("groups"), lax.axis_size("tile")
+    smem = pl.BlockSpec(memory_space=pltpu.SMEM)
+    vmem = pl.BlockSpec(memory_space=pltpu.VMEM)
+    hbm = pl.BlockSpec(memory_space=pl.ANY)
+    dma = pltpu.SemaphoreType.DMA
+    piece = pltpu.VMEM((CHUNKS, e // CHUNKS, e), F32)
+    return pl.pallas_call(
+        functools.partial(share_kernel, groups, tiles_n),
+        out_shape=(jax.ShapeDtypeStruct((slabs, e, e), F32), jax.ShapeDtypeStruct((layers, e, cols), F32)),
+        in_specs=[smem, smem, vmem, hbm],
+        out_specs=(vmem, hbm),
+        scratch_shapes=[
+            pltpu.VMEM((PLANE, e, e), F32), pltpu.VMEM((PLANE - 1, e, e), F32), pltpu.VMEM((e, e), F32),
+            piece, piece, piece, piece,
+            pltpu.VMEM((slabs, e, e), F32), pltpu.VMEM((layers, e, cols), F32),
+            dma((PLANE - 1,)), dma((PLANE - 1,)), dma((CHUNKS,)), dma((CHUNKS,)), dma((CHUNKS,)), dma((CHUNKS,)),
+            dma((3, CHUNKS)), dma((3, CHUNKS)), dma((4, CHUNKS)), dma((4, CHUNKS)), dma, dma, dma,
+        ],
+        compiler_params=pltpu.CompilerParams(collective_id=0, has_side_effects=True),
+    )(block_owner, block_clips, library, tiles)
+
+
+def peak_kernel(tiles_n, per_block, peaks, out, slots, send, recv):
+    g = lax.axis_index("groups")
+    t = lax.axis_index("tile")
+    others = [(g, lax.rem(t + d, tiles_n)) for d in range(1, tiles_n)]
+    barrier = pltpu.get_barrier_semaphore()
+    for target in others:
+        pl.semaphore_signal(barrier, inc=1, device_id=target, device_id_type=MESH)
+    pl.semaphore_wait(barrier, tiles_n - 1)
+    copies = []
+    for n, target in enumerate(others):
+        copy = pltpu.make_async_remote_copy(src_ref=peaks, dst_ref=slots.at[n], send_sem=send.at[n],
+                                            recv_sem=recv.at[n], device_id=target, device_id_type=MESH)
+        copy.start()
+        copies.append(copy)
+    best = peaks[...]
+    for n, copy in enumerate(copies):
+        copy.wait_recv()
+        best = jnp.maximum(best, slots[n])
+    best = jnp.max(best, axis=1, keepdims=True)
+    for k in range(out.shape[0] * per_block):
+        at = k % per_block
+        out[k // per_block:k // per_block + 1, at:at + 1] = best[k:k + 1]
+    for copy in copies:
+        copy.wait_send()
+
+
+def share_peaks(peaks, shape):
+    tiles_n = lax.axis_size("tile")
+    vmem = pl.BlockSpec(memory_space=pltpu.VMEM)
+    dma = pltpu.SemaphoreType.DMA
+    return pl.pallas_call(
+        functools.partial(peak_kernel, tiles_n, shape[1]),
+        out_shape=jax.ShapeDtypeStruct(shape, F32),
+        in_specs=[vmem],
+        out_specs=vmem,
+        scratch_shapes=[pltpu.VMEM((tiles_n - 1,) + peaks.shape, F32), dma((tiles_n - 1,)), dma((tiles_n - 1,))],
+        compiler_params=pltpu.CompilerParams(collective_id=1, has_side_effects=True),
+    )(peaks)
+
+
 def local(tiles, library, block_owner, block_clips, layer_order):
-    e = library.shape[-1]
-    halo = from_behind(tiles[:, :e, :], "tile")
-    picked = library[block_clips]
-    owned = block_owner == lax.axis_index("tile")
-    delivered = lax.psum(jnp.where(owned[:, None, None, None, None], picked, 0.0), "tile")
-    scores, peaks = correlate(tiles, halo, delivered, layer_order)
-    peak = lax.pmax(jnp.max(peaks, axis=1), "tile").reshape(block_clips.shape)
-    return scores, peak
+    layers, e = library.shape[1], library.shape[-1]
+    delivered, halo = share(tiles, library, block_owner, block_clips)
+    clips = delivered.reshape(block_clips.shape + (layers, e, e))
+    scores, peaks = correlate(tiles, halo, clips, layer_order)
+    return scores, share_peaks(peaks, block_clips.shape)
 
 
 def solution(mesh):

time: 165 us -> 56.7 us (0.34)
  waiting for transfers between devices: 94.4 us -> 0 us
  Pallas kernels: 17 us -> 54.6 us
  blocking collectives: 32.4 us -> 0 us
  between operations: 14.1 us -> 0.65 us
  other arithmetic: 3.04 us -> 0 us
    psum x1 -> x0, waiting for transfers between devices: 94.4 us -> none  [local(): lax.psum(jnp.where(owned[:, None, None, None, None], picked, 0.0), 'tile')]
    pallas_call x0 -> x2, Pallas kernels: none -> 37.7 us  [the longest x1 29.6 us: share(): pl.pallas_call(functools.partial(share_kernel, groups, tiles_n), out_shap...]
    pmax x1 -> x0, blocking collectives: 32.4 us -> none  [local(): peak = lax.pmax(jnp.max(peaks, axis=1), 'tile').reshape(block_clips.shape)]
  transfers between devices with their start and end apart: 2 -> 0, of which waited for: 1 -> 0; matrix products, arithmetic and copies ran while one was open for 2% -> 0% of each run, Pallas kernels for 0% -> 0%
where the time goes in v1:
time: 56.7 us; the launch traced here: 56.5 us
  Pallas kernels  54.6 us (96%)
  local copies, waits for them, and re-layouts  1.22 us (2%)
  between operations  0.65 us (1%)
    pallas_call x1, Pallas kernels, share(): pl.pallas_call(functools.partial(share_kernel, groups, tiles_n), out_shap...  29.6 us
    pallas_call x1, Pallas kernels, correlate(): pl.pallas_call(kernel, out_shape=(jax.ShapeDtypeStruct((blocks, per_block...  16.9 us
    pallas_call x1, Pallas kernels, share_peaks(): pl.pallas_call(functools.partial(peak_kernel, tiles_n, shape[1]), out_sha...  8.1 us
    unnamed x1, local copies, waits for them, and re-layouts  1.22 us

profile of v1, /device:TPU:0, one launch (start us, length us, event | category | flops | bytes accessed | tf_op | source)
XLA Modules:
  0.0 56.5 jit_solution(16462278369700323548)
XLA Ops:
  0.6 29.6 %shard_map.122 = (f32[8,128,128]{2,1,0:T(8,128)}, f32[2,128,384]{2,1,0:T(8,128)}) custom-call(s32[2]{0:T(128)} %owner.1, s32[2,2]{1,0:T(2,128)} %picks.1, f32[8,2,128,128]{3,2,1,0:T(8,128)} %library.1, f32[2,384,384]{2,1,0:T(8,128)} %tiles.3), custom_call_target="tpu_custom_call" | custom-call | tf_op jit(solution)/shard_map/pallas_call | solution.py:354
  30.2 16.9 %shard_map.123 = (f32[2,2,384,384]{3,2,1,0:T(8,128)}, f32[8,128]{1,0:T(8,128)}) custom-call(s32[1,2]{1,0:T(1,128)} %order.1, f32[2,384,384]{2,1,0:T(8,128)} %tiles.3, f32[2,128,384]{2,1,0:T(8,128)} %get-tuple-element.6.halo, f32[2,2,2,128,128]{4,3,2,1,0:T(8,128)} %bitcast.1, bf16[256,768]{1,0:T(8,128)(2,1)} %constant.12.clone.row_left, ...), custom_call_target="tpu_custom_call" | custom-call | tf_op jit(solution)/shard_map/pallas_call | solution.py:160
  47.1 8.1 %shard_map.124 = f32[2,2]{1,0:T(2,128)} custom-call(f32[8,128]{1,0:T(8,128)} %get-tuple-element.9.peaks), custom_call_target="tpu_custom_call" | custom-call | tf_op jit(solution)/shard_map/pallas_call | solution.py:400
  55.2 1.2 %copy.14 = f32[2,2]{1,0:T(2,128)} copy(f32[2,2]{1,0:T(2,128)} %shard_map.124) | data formatting | bytes 32

commit v2 on v1

v2 whole, which is shorter than its diff:
```python
import functools
import math

import jax
import jax.numpy as jnp
import numpy as np
from jax import lax
from jax.experimental import pallas as pl
from jax.experimental.pallas import tpu as pltpu
from jax.sharding import PartitionSpec as P

F32 = jnp.float32
BF16 = jnp.bfloat16


def split(x):
    high = x.astype(BF16)
    return high, (x - high.astype(F32)).astype(BF16)


def mm(a, b):
    return jnp.dot(a, b, preferred_element_type=F32)


def transform_matrix(extent):
    span = 2 * extent
    odd = 2 * np.arange(extent)[:, None] + 1
    angle = (odd * np.arange(span)[None, :] % (2 * span)) * (math.pi / span)
    return np.concatenate([np.cos(angle), np.sin(angle)], axis=0).astype(np.float32)


def halves(matrix):
    high = matrix.astype(BF16)
    low = (matrix - high.astype(np.float32)).astype(BF16)
    return high, low


def constants(extent):
    forward = transform_matrix(extent)
    fh, fl = halves(forward)
    row_left = np.concatenate([fh, fl, fh], axis=1)
    ft = np.ascontiguousarray(forward.T)
    th, tl = halves(ft)
    col_right = np.stack([th, tl])
    back = forward[:, :extent] * np.float32(1.0 / extent)
    bh, bl = halves(back)
    back_right = np.stack([bh, bl])
    back_left = np.concatenate([bh.T, bl.T, bh.T], axis=1)
    offset = np.arange(2 * extent)[None, :] - np.arange(extent)[:, None]
    band = ((offset >= 0) & (offset < extent)).astype(BF16)
    band_left = np.concatenate([band, band], axis=1)
    band_right = np.ascontiguousarray(band.T)
    return [jnp.asarray(c) for c in (row_left, col_right, back_left, back_right, band_left, band_right)]


def combine(y, e):
    a, b = y[:e, :e], y[:e, e:]
    c, d = y[e:, :e], y[e:, e:]
    return a - d, b + c, a + d, c - b


class Transforms:
    def __init__(self, refs, shapes):
        self.__dict__.update(refs)
        self.layers, self.rows, self.cols, self.e, self.per_block, self.count = shapes
        self.span = 2 * self.e
        self.nc = self.cols // self.e
        self.entries = self.layers * self.e * self.e

    def rows_of(self, b, window):
        e, squares = self.e, None
        for l in range(self.layers):
            x = window(l)
            squares = x * x if squares is None else squares + x * x
            xh, xl = split(x)
            y = mm(self.row_left[...], jnp.concatenate([xh, xh, xl], axis=0))
            h, low = split(y)
            self.yh[l], self.yl[l] = h, low
        sh, sl = split(squares)
        energy = mm(self.band_left[...], jnp.concatenate([sh, sl], axis=0))
        eh, el = split(energy)
        for c in range(self.nc):
            width = min(2, self.nc - c) * e
            at = slice(c * e, c * e + width)
            total = mm(eh[:, at], self.band_right[:width]) + mm(el[:, at], self.band_right[:width])
            self.inv[b, :, c * e:(c + 1) * e] = 1.0 / jnp.sqrt(total / self.entries + 1e-05)

    def columns_of(self, b):
        e = self.e
        for c in range(self.nc):
            width = min(2, self.nc - c) * e
            at = slice(c * e, c * e + width)
            for l in range(self.layers):
                h, low = self.yh[l, :, at], self.yl[l, :, at]
                y = mm(h, self.col_right[0, :width]) + mm(low, self.col_right[0, :width]) + mm(h, self.col_right[1, :width])
                for n, part in enumerate(combine(y, e)):
                    self.tile_parts[b, c, l, n] = part

    def clip_of(self, k, layer_at):
        e, span, row_left, col_right = self.e, self.span, self.row_left, self.col_right
        total = jnp.zeros((e, e), F32)
        for l in range(self.layers):
            chosen = layer_at(l)
            total = total + chosen * chosen
            ch, cl = split(chosen)
            first = mm(row_left[:, :e], ch) + mm(row_left[:, span:span + e], ch) + mm(row_left[:, :e], cl)
            fh, fl = split(first)
            second = mm(fh, col_right[0, :e]) + mm(fl, col_right[0, :e]) + mm(fh, col_right[1, :e])
            for n, part in enumerate(combine(second, e)):
                self.spectra[k, l, n] = part
        mean = jnp.sum(total, keepdims=True) / self.entries
        return 1.0 / (math.sqrt(self.entries) * jnp.sqrt(mean + 1e-05))

    def inverse_of(self, b, clip_scale):
        e = self.e
        for c in range(self.nc):
            for k in range(self.count):
                u1 = u2 = v1 = v2 = None
                for l in range(self.layers):
                    p1, p2, q1, q2 = (self.tile_parts[b, c, l, n] for n in range(4))
                    c1, c2, d1, d2 = (self.spectra[k, l, n] for n in range(4))
                    t = (p1 * c1 + p2 * c2, p2 * c1 - p1 * c2, q1 * d1 + q2 * d2, q2 * d1 - q1 * d2)
                    if u1 is None:
                        u1, u2, v1, v2 = t
                    else:
                        u1, u2, v1, v2 = u1 + t[0], u2 + t[1], v1 + t[2], v2 + t[3]
                z = jnp.concatenate([
                    jnp.concatenate([u1 + v1, u2 - v2], axis=1),
                    jnp.concatenate([u2 + v2, v1 - u1], axis=1)], axis=0)
                zh, zl = split(z)
                w = mm(zh, self.back_right[0]) + mm(zl, self.back_right[0]) + mm(zh, self.back_right[1])
                h, low = split(w)
                self.wh[k, :, c * e:(c + 1) * e] = h
                self.wl[k, :, c * e:(c + 1) * e] = low
        scale = self.inv[b]
        for k in range(self.count):
            out = mm(self.back_left[...], jnp.concatenate([self.wh[k], self.wh[k], self.wl[k]], axis=0))
            out = out * scale * (clip_scale[k] * 0.5)
            self.scores[k // self.per_block, k % self.per_block, pl.ds(pl.multiple_of(b * e, e), e)] = out
            top = jnp.max(out, axis=0, keepdims=True)
            best = self.peaks[k:k + 1]
            for c in range(self.nc):
                best = jnp.maximum(best, top[:, c * e:(c + 1) * e])
            self.peaks[k:k + 1] = best


MESH = pl.DeviceIdType.MESH
PLANE = 4
CHUNKS = 4


def kernel(tiles_n, owner, picks, order, library, tiles, row_left, col_right, back_left, back_right,
           band_left, band_right, scores, peak_out,
           yh, yl, inv, tile_parts, spectra, wh, wl, peaks, slots,
           stage, landed, mine, rbuf, lbuf, rsend, lsend, full, halo_in,
           rs_send, rs_recv, r_send, r_recv, l_send, l_recv,
           ag_send, ag_recv, fw_send, fw_recv, halo_send, halo_recv, peak_send, peak_recv):
    g = lax.axis_index("groups")
    t = lax.axis_index("tile")
    per_block = picks.shape[1]
    layers, rows, cols = tiles.shape
    e = library.shape[-1]
    nr = rows // e
    count = picks.shape[0] * per_block
    work = Transforms(dict(row_left=row_left, col_right=col_right, back_left=back_left, back_right=back_right,
                           band_left=band_left, band_right=band_right, scores=scores, yh=yh, yl=yl, inv=inv,
                           tile_parts=tile_parts, spectra=spectra, wh=wh, wl=wl, peaks=peaks),
                      (layers, rows, cols, e, per_block, count))
    z = t // PLANE
    q = lax.rem(t, PLANE)
    depth = tiles_n // PLANE
    parity = lax.rem(g, 2)
    other_g = g + 1 - 2 * parity
    core = lax.rem(q, 2)
    partner = t + 1 - 2 * core
    upper = q // 2
    across = t + 2 - 4 * upper
    plane = [z * PLANE + lax.rem(q + d, PLANE) for d in range(1, PLANE)]
    others = [(g, lax.rem(t + d, tiles_n)) for d in range(1, tiles_n)]
    greeted = others + [(other_g, t), (other_g, across)]

    barrier = pltpu.get_barrier_semaphore()
    for target in greeted:
        pl.semaphore_signal(barrier, inc=1, device_id=target, device_id_type=MESH)

    def contribution(slab):
        clip, layer = slab // layers, lax.rem(slab, layers)
        block, which = clip // per_block, lax.rem(clip, per_block)
        mask = jnp.where(owner[block] == t, 1.0, 0.0).astype(F32)
        return library[picks[block, which], layer] * mask

    for d in range(PLANE):
        stage[d] = contribution(parity * PLANE + lax.rem(q + d, PLANE))

    @pl.when(z == 0)
    def _():
        rbuf[...] = jnp.zeros_like(rbuf)

    @pl.when(z == depth - 1)
    def _():
        lbuf[...] = jnp.zeros_like(lbuf)

    @pl.when(t == tiles_n - 1)
    def _():
        halo_in[...] = jnp.zeros_like(halo_in)

    peaks[...] = jnp.full(peaks.shape, -jnp.inf, F32)
    pl.semaphore_wait(barrier, len(greeted))

    def remote(src, dst, send, recv, target):
        return pltpu.make_async_remote_copy(src_ref=src, dst_ref=dst, send_sem=send, recv_sem=recv,
                                            device_id=target, device_id_type=MESH)

    scatter = []
    for d in range(1, PLANE):
        copy = remote(stage.at[d], landed.at[d - 1], rs_send.at[d - 1], rs_recv.at[d - 1], (g, plane[d - 1]))
        copy.start()
        scatter.append(copy)
    work.rows_of(0, lambda l: tiles[l, :2 * e])
    for copy in scatter:
        copy.wait()
    mine[...] = stage[0] + landed[0] + landed[1] + landed[2]

    step = e // CHUNKS
    parts = [pl.ds(c * step, step) for c in range(CHUNKS)]
    slab = parity * PLANE + q
    right = [remote(rsend.at[c], rbuf.at[c], r_send.at[c], r_recv.at[c], (g, t + PLANE)) for c in range(CHUNKS)]
    left = [remote(lsend.at[c], lbuf.at[c], l_send.at[c], l_recv.at[c], (g, t - PLANE)) for c in range(CHUNKS)]
    forwards = []
    slabs = [slab, (1 - parity) * PLANE + q,
             parity * PLANE + q + 2 - 4 * upper, (1 - parity) * PLANE + q + 2 - 4 * upper]
    targets = [(other_g, t), (g, across), (other_g, across)]

    def forward(n, c):
        copy = remote(full.at[slabs[n], parts[c]], full.at[slabs[n], parts[c]],
                      fw_send.at[n, c], fw_recv.at[n, c], (g, partner))
        copy.start()
        forwards.append(copy)

    gathers = [(n, c, remote(full.at[slab, parts[c]], full.at[slab, parts[c]], ag_send.at[n, c], ag_recv.at[n, c], target))
               for c in range(CHUNKS) for n, target in enumerate(targets)]
    own = [remote(full.at[slab, parts[c]], full.at[slab, parts[c]], fw_send.at[0, c], fw_recv.at[0, c], (g, partner))
           for c in range(CHUNKS)]

    def rightward(c):
        @pl.when(z > 0)
        def _():
            right[c].wait_recv()
        rsend[c] = rbuf[c] + mine[parts[c]]

        @pl.when(z < depth - 1)
        def _():
            right[c].start()

    def leftward(c):
        @pl.when(z < depth - 1)
        def _():
            left[c].wait_recv()
        lsend[c] = lbuf[c] + mine[parts[c]]

        @pl.when(z > 0)
        def _():
            left[c].start()

    def deliver(c):
        full[slab, parts[c]] = rsend[c] + lbuf[c]
        for n in range(3):
            gathers[3 * c + n][2].start()
        own[c].start()

    lower = z < depth // 2
    for condition, first, second in ((lower, rightward, leftward), (jnp.logical_not(lower), leftward, rightward)):
        @pl.when(condition)
        def _(first=first, second=second):
            for c in range(CHUNKS):
                first(c)
            for c in range(CHUNKS):
                second(c)
                deliver(c)
    forwards.extend(own)
    work.columns_of(0)
    work.rows_of(1, lambda l: tiles[l, e:3 * e])
    for n, c, copy in gathers:
        copy.wait_recv()
        forward(n + 1, c)
    halo = remote(tiles.at[:, pl.ds(0, e)], halo_in, halo_send, halo_recv, (g, t - 1))

    @pl.when(t > 0)
    def _():
        halo.start()

    for b in range(1, nr - 1):
        if b > 1:
            work.rows_of(b, lambda l: tiles[l, b * e:(b + 2) * e])
        work.columns_of(b)
    for copy in forwards:
        copy.wait_recv()
    clip_scale = [work.clip_of(k, lambda l: full[k * layers + order[0, l]]) for k in range(count)]

    def row_block(b, carry):
        @pl.when(b == nr - 1)
        def _():
            @pl.when(t < tiles_n - 1)
            def _():
                halo.wait_recv()
            work.rows_of(nr - 1, lambda l: jnp.concatenate([tiles[l, rows - e:], halo_in[l]], axis=0))
            work.columns_of(nr - 1)
        work.inverse_of(b, clip_scale)
        return carry

    lax.fori_loop(0, nr, row_block, 0)

    copies = [remote(peaks, slots.at[n], peak_send.at[n], peak_recv.at[n], target) for n, target in enumerate(others)]
    for copy in copies:
        copy.start()
    for _, _, copy in gathers:
        copy.wait_send()
    for copy in forwards:
        copy.wait_send()
    for c in range(CHUNKS):
        @pl.when(z < depth - 1)
        def _(c=c):
            right[c].wait_send()

        @pl.when(z > 0)
        def _(c=c):
            left[c].wait_send()

    @pl.when(t > 0)
    def _():
        halo.wait_send()

    best = peaks[...]
    for n, copy in enumerate(copies):
        copy.wait_recv()
        best = jnp.maximum(best, slots[n])
    best = jnp.max(best, axis=1, keepdims=True)
    for k in range(count):
        at = k % per_block
        peak_out[k // per_block:k // per_block + 1, at:at + 1] = best[k:k + 1]
    for copy in copies:
        copy.wait_send()


def local(tiles, library, block_owner, block_clips, layer_order):
    layers, rows, cols = tiles.shape
    e = library.shape[-1]
    span, nr, nc = 2 * e, rows // e, cols // e
    blocks, per_block = block_clips.shape
    count = blocks * per_block
    slabs = count * layers
    assert slabs == 2 * PLANE
    tiles_n = lax.axis_size("tile")
    smem = pl.BlockSpec(memory_space=pltpu.SMEM)
    vmem = pl.BlockSpec(memory_space=pltpu.VMEM)
    dma = pltpu.SemaphoreType.DMA
    piece = pltpu.VMEM((CHUNKS, e // CHUNKS, e), F32)
    lines = -(-count // 8) * 8
    return pl.pallas_call(
        functools.partial(kernel, tiles_n),
        out_shape=(jax.ShapeDtypeStruct((blocks, per_block, rows, cols), F32),
                   jax.ShapeDtypeStruct((blocks, per_block), F32)),
        in_specs=[smem] * 3 + [vmem] * 8,
        out_specs=(vmem, vmem),
        scratch_shapes=[
            pltpu.VMEM((layers, span, cols), BF16), pltpu.VMEM((layers, span, cols), BF16),
            pltpu.VMEM((nr, e, cols), F32),
            pltpu.VMEM((nr, nc, layers, 4, e, e), F32), pltpu.VMEM((count, layers, 4, e, e), F32),
            pltpu.VMEM((count, span, cols), BF16), pltpu.VMEM((count, span, cols), BF16),
            pltpu.VMEM((lines, e), F32), pltpu.VMEM((tiles_n - 1, lines, e), F32),
            pltpu.VMEM((PLANE, e, e), F32), pltpu.VMEM((PLANE - 1, e, e), F32), pltpu.VMEM((e, e), F32),
            piece, piece, piece, piece,
            pltpu.VMEM((slabs, e, e), F32), pltpu.VMEM((layers, e, cols), F32),
            dma((PLANE - 1,)), dma((PLANE - 1,)), dma((CHUNKS,)), dma((CHUNKS,)), dma((CHUNKS,)), dma((CHUNKS,)),
            dma((3, CHUNKS)), dma((3, CHUNKS)), dma((4, CHUNKS)), dma((4, CHUNKS)), dma, dma,
            dma((tiles_n - 1,)), dma((tiles_n - 1,)),
        ],
        compiler_params=pltpu.CompilerParams(collective_id=0, has_side_effects=True, vmem_limit_bytes=60 * 1024 * 1024),
    )(block_owner, block_clips, layer_order, library, tiles, *constants(e))


def solution(mesh):
    in_specs = (
        P(None, ("groups", "tile"), None),
        P("tile", None, None, None),
        P(),
        P(),
        P(("groups", "tile"), None),
    )
    out_specs = (P(None, None, ("groups", "tile"), None), P("groups", None))
    return jax.shard_map(local, mesh=mesh, in_specs=in_specs, out_specs=out_specs, check_vma=False)
```

time: 56.7 us -> 47.6 us (0.84)
  Pallas kernels: 54.6 us -> 43 us
  local copies, waits for them, and re-layouts: 1.22 us -> 3.79 us
    pallas_call x3 -> x1, Pallas kernels: 54.6 us -> 43 us  [local(): pl.pallas_call(functools.partial(kernel, tiles_n), out_shape=(jax.ShapeDt...]
    unnamed x1 -> x4, local copies, waits for them, and re-layouts: 1.22 us -> 3.79 us
where the time goes in v2:
time: 47.6 us; the launch traced here: 47.4 us
  Pallas kernels  43 us (90%)
  local copies, waits for them, and re-layouts  3.79 us (8%)
  between operations  0.65 us (1%)
    pallas_call x1, Pallas kernels, local(): pl.pallas_call(functools.partial(kernel, tiles_n), out_shape=(jax.ShapeDt...  43 us
    unnamed x4, local copies, waits for them, and re-layouts  3.79 us

profile of v2, /device:TPU:0, one launch (start us, length us, event | category | flops | bytes accessed | tf_op | source)
XLA Modules:
  0.0 47.4 jit_solution(2117847038444868352)
XLA Ops:
  0.6 43.0 %shard_map.122 = (f32[2,2,384,384]{3,2,1,0:T(8,128)}, f32[2,2]{1,0:T(2,128)}) custom-call(s32[2]{0:T(128)} %owner.1, s32[2,2]{1,0:T(2,128)} %picks.1, s32[1,2]{1,0:T(1,128)} %order.1, f32[8,2,128,128]{3,2,1,0:T(8,128)} %library.1, f32[2,384,384]{2,1,0:T(8,128)} %tiles.1, bf16[256,768]{1,0:T(8,128)(2,1)} %constant.12.clone.row_left, ...), custom_call_target="tpu_custom_call" | custom-call | tf_op jit(solution)/shard_map/pallas_call | solution.py:359
  43.6 0.0 copy-start
  43.6 3.2 %copy.15 = f32[2,2,384,384]{3,2,1,0:T(8,128)} copy(f32[2,2,384,384]{3,2,1,0:T(8,128)} %get-tuple-element.4) | data formatting | bytes 4718592
  46.8 0.0 copy-done
  46.8 0.6 %copy.16 = f32[2,2]{1,0:T(2,128)} copy(f32[2,2]{1,0:T(2,128)S(1)} %copy-done) | data formatting | bytes 32
Async XLA Ops:
  43.6 3.2 %copy-start = (f32[2,2]{1,0:T(2,128)S(1)}, f32[2,2]{1,0:T(2,128)}, u32[]{:S(2)}) copy-start(f32[2,2]{1,0:T(2,128)} %get-tuple-element.5) | copy-start | bytes 52

commit v3 on v2

--- a/solution.py
+++ b/solution.py
@@ -149,12 +149,18 @@
 CHUNKS = 4
 
 
-def kernel(tiles_n, owner, picks, order, library, tiles, row_left, col_right, back_left, back_right,
-           band_left, band_right, scores, peak_out,
+def kernel(tiles_n, owner, picks, order, *refs):
+    sources = refs[:8]
+    (scores, peak_out,
            yh, yl, inv, tile_parts, spectra, wh, wl, peaks, slots,
            stage, landed, mine, rbuf, lbuf, rsend, lsend, full, halo_in,
            rs_send, rs_recv, r_send, r_recv, l_send, l_recv,
-           ag_send, ag_recv, fw_send, fw_recv, halo_send, halo_recv, peak_send, peak_recv):
+           ag_send, ag_recv, fw_send, fw_recv, halo_send, halo_recv, peak_send, peak_recv,
+           library, tiles, row_left, col_right, back_left, back_right, band_left, band_right, load_sem) = refs[8:]
+    loads = [pltpu.make_async_copy(a, b, load_sem.at[n]) for n, (a, b) in enumerate(zip(
+        sources, (library, tiles, row_left, col_right, back_left, back_right, band_left, band_right)))]
+    for load in loads:
+        load.start()
     g = lax.axis_index("groups")
     t = lax.axis_index("tile")
     per_block = picks.shape[1]
@@ -183,6 +189,8 @@
     for target in greeted:
         pl.semaphore_signal(barrier, inc=1, device_id=target, device_id_type=MESH)
 
+    loads[0].wait()
+
     def contribution(slab):
         clip, layer = slab // layers, lax.rem(slab, layers)
         block, which = clip // per_block, lax.rem(clip, per_block)
@@ -216,6 +224,8 @@
         copy = remote(stage.at[d], landed.at[d - 1], rs_send.at[d - 1], rs_recv.at[d - 1], (g, plane[d - 1]))
         copy.start()
         scatter.append(copy)
+    for load in loads[1:]:
+        load.wait()
     work.rows_of(0, lambda l: tiles[l, :2 * e])
     for copy in scatter:
         copy.wait()
@@ -356,11 +366,12 @@
     dma = pltpu.SemaphoreType.DMA
     piece = pltpu.VMEM((CHUNKS, e // CHUNKS, e), F32)
     lines = -(-count // 8) * 8
+    operands = [library, tiles, *constants(e)]
     return pl.pallas_call(
         functools.partial(kernel, tiles_n),
         out_shape=(jax.ShapeDtypeStruct((blocks, per_block, rows, cols), F32),
                    jax.ShapeDtypeStruct((blocks, per_block), F32)),
-        in_specs=[smem] * 3 + [vmem] * 8,
+        in_specs=[smem] * 3 + [pl.BlockSpec(memory_space=pltpu.HBM)] * 8,
         out_specs=(vmem, vmem),
         scratch_shapes=[
             pltpu.VMEM((layers, span, cols), BF16), pltpu.VMEM((layers, span, cols), BF16),
@@ -374,9 +385,9 @@
             dma((PLANE - 1,)), dma((PLANE - 1,)), dma((CHUNKS,)), dma((CHUNKS,)), dma((CHUNKS,)), dma((CHUNKS,)),
             dma((3, CHUNKS)), dma((3, CHUNKS)), dma((4, CHUNKS)), dma((4, CHUNKS)), dma, dma,
             dma((tiles_n - 1,)), dma((tiles_n - 1,)),
-        ],
+        ] + [pltpu.VMEM(a.shape, a.dtype) for a in operands] + [dma((len(operands),))],
         compiler_params=pltpu.CompilerParams(collective_id=0, has_side_effects=True, vmem_limit_bytes=60 * 1024 * 1024),
-    )(block_owner, block_clips, layer_order, library, tiles, *constants(e))
+    )(block_owner, block_clips, layer_order, *operands)
 
 
 def solution(mesh):

time: 47.6 us -> 46.5 us (0.977)
  Pallas kernels: 43 us -> 41.9 us
    pallas_call x1, Pallas kernels: 43 us -> 41.9 us  [local(): pl.pallas_call(functools.partial(kernel, tiles_n), out_shape=(jax.ShapeDt...]
where the time goes in v3:
time: 46.5 us; the launch traced here: 46.3 us
  Pallas kernels  41.9 us (90%)
  local copies, waits for them, and re-layouts  3.79 us (8%)
  between operations  0.65 us (1%)
    pallas_call x1, Pallas kernels, local(): pl.pallas_call(functools.partial(kernel, tiles_n), out_shape=(jax.ShapeDt...  41.9 us
    unnamed x4, local copies, waits for them, and re-layouts  3.79 us

profile of v3, /device:TPU:0, one launch (start us, length us, event | category | flops | bytes accessed | tf_op | source)
XLA Modules:
  0.0 46.3 jit_solution(10190116596824339276)
XLA Ops:
  0.6 41.9 %shard_map.122 = (f32[2,2,384,384]{3,2,1,0:T(8,128)}, f32[2,2]{1,0:T(2,128)}) custom-call(s32[2]{0:T(128)} %owner.1, s32[2,2]{1,0:T(2,128)} %picks.1, s32[1,2]{1,0:T(1,128)} %order.1, f32[8,2,128,128]{3,2,1,0:T(8,128)} %refs_0_.1, f32[2,384,384]{2,1,0:T(8,128)} %refs_1_.1, bf16[256,768]{1,0:T(8,128)(2,1)} %constant.12.clone.refs_2_, ...), custom_call_target="tpu_custom_call" | custom-call | tf_op jit(solution)/shard_map/pallas_call | solution.py:370
  42.5 0.0 copy-start
  42.5 3.2 %copy.15 = f32[2,2,384,384]{3,2,1,0:T(8,128)} copy(f32[2,2,384,384]{3,2,1,0:T(8,128)} %get-tuple-element.4) | data formatting | bytes 4718592
  45.7 0.0 copy-done
  45.7 0.6 %copy.16 = f32[2,2]{1,0:T(2,128)} copy(f32[2,2]{1,0:T(2,128)S(1)} %copy-done) | data formatting | bytes 32
Async XLA Ops:
  42.5 3.2 %copy-start = (f32[2,2]{1,0:T(2,128)S(1)}, f32[2,2]{1,0:T(2,128)}, u32[]{:S(2)}) copy-start(f32[2,2]{1,0:T(2,128)} %get-tuple-element.5) | copy-start | bytes 52
